TPU v7x, 32 devices: a whole 2x2x4 slice. The times are simulated.
32 devices in a mesh: tm: 8 (over y, x, core), sector: 4 (over z).
Axes of the slice: x: 2, y: 2, z: 4, core: 2. Of those that a mesh axis runs over, the one named last changes fastest.
Arguments:
- propagator: bfloat16 [4, 8, 640, 640], P('sector', 'tm'), may hold values from -6 to 6
- rising_op: bfloat16 [4, 640, 640], P('sector'), may hold values from -0.25 to 0.25
- energies: float32 [4, 640], P('sector'), may hold values from 0.5 to 40
- hyb_particle: float32 [8], P('tm'), may hold values from 0.2 to 1
- hyb_hole: float32 [8], P('tm'), may hold values from 0.2 to 1
- sector_sizes: int32 [4], P('sector'), may hold values from 160 to 640, as said below
Outputs:
- new_prop: bfloat16 [4, 8, 640, 640], P('sector', 'tm')
Inputs may be any that keep to these rules, and one draw needn't show every extreme that they name: `sector_sizes`: one sector holds exactly 640 states.
All inputs are finite; a program needn't handle non-finite values.
Results may differ from a plain program's by a relative error of at most 0.0061.
Values may be sent and summed in bfloat16 or wider, within the bound.
A program may use at most 128 MiB of HBM per device.

v0:
```python
import jax
import jax.numpy as jnp
from jax import lax
from jax.sharding import PartitionSpec as P


def shifted(block, axis, distance):
    devices = range(lax.axis_size(axis))
    route = [(i - distance, i) for i in devices if i - distance in devices]
    return lax.ppermute(block, axis, route)


def per_device(propagator, rising_op, energies, hyb_particle, hyb_hole, sector_sizes):
    t_dev = propagator.shape[1]
    states = propagator.shape[2]
    time_count = t_dev * lax.axis_size("tm")
    step_size = 1.0 / time_count
    positions = jnp.arange(states, dtype=jnp.int32)
    live_mask = positions < sector_sizes[0]
    square = live_mask[:, None] & live_mask[None, :]
    masked_prop = jnp.where(square[None], propagator[0], jnp.zeros((), jnp.bfloat16))
    operator = rising_op[0]
    raised = jnp.einsum(
        "ik,tkl->til", operator, masked_prop, preferred_element_type=jnp.float32
    ).astype(jnp.bfloat16)
    upward = jnp.einsum("tik,jk->tij", raised, operator, preferred_element_type=jnp.float32).astype(
        jnp.bfloat16
    )
    from_below = shifted(upward, "sector", 1)
    from_above = shifted(masked_prop, "sector", -1)
    lowered = jnp.einsum(
        "ki,tkl->til", operator, from_above, preferred_element_type=jnp.float32
    ).astype(jnp.bfloat16)
    downward = jnp.einsum("tik,kl->til", lowered, operator, preferred_element_type=jnp.float32)
    combined = (
        hyb_particle[:, None, None] * from_below.astype(jnp.float32)
        + hyb_hole[:, None, None] * downward
    )
    self_energy = jnp.where(square[None], combined, jnp.zeros((), jnp.float32)).astype(jnp.bfloat16)
    rows_each = states // lax.axis_size("tm")
    first_row = lax.axis_index("tm") * rows_each
    lag_rows = lax.all_to_all(self_energy, "tm", split_axis=1, concat_axis=0, tiled=True)
    history = lax.all_gather(masked_prop, "tm", axis=0, tiled=True)
    mirrored = jnp.concatenate([history[::-1], history], 0)
    slots = jnp.arange(time_count, dtype=jnp.int32)
    wide_slots = jnp.arange(time_count + 1, dtype=jnp.int32)

    def pair_step(lag, sums):
        forward, backward = sums
        other = time_count - 1 - lag
        window = lax.dynamic_slice_in_dim(mirrored, lag, time_count + 1, 0)
        near = lax.dynamic_index_in_dim(lag_rows, lag, 0, keepdims=False)
        far = lax.dynamic_index_in_dim(lag_rows, other, 0, keepdims=False)
        left = jnp.where((wide_slots < time_count - lag)[:, None, None], near[None], far[None])
        product = jnp.einsum("uik,ukl->uil", left, window, preferred_element_type=jnp.float32)
        backward = backward + jnp.where(
            (slots < time_count - lag)[:, None, None],
            product[:time_count],
            jnp.zeros((), jnp.float32),
        )
        forward = forward + jnp.where(
            (slots >= time_count - lag - 1)[:, None, None], product[1:], jnp.zeros((), jnp.float32)
        )
        return (forward, backward)

    empty_rows = jnp.zeros((time_count, rows_each, states), jnp.float32)
    forward, backward = lax.fori_loop(0, time_count // 2, pair_step, (empty_rows, empty_rows))
    convolved = step_size * (forward + backward[::-1])
    row_ids = first_row + jnp.arange(rows_each, dtype=jnp.int32)
    row_rates = lax.dynamic_slice_in_dim(energies[0], first_row, rows_each, 0)
    decay_rows = jnp.exp(-step_size * row_rates)

    def advance(running, term):
        running = decay_rows[:, None] * running + term
        return (running, running)

    _, summed = lax.scan(advance, jnp.zeros((rows_each, states), jnp.float32), convolved)
    moments = jnp.arange(time_count).astype(jnp.float32) * step_size
    live_rows = row_ids < sector_sizes[0]
    free_part = jnp.where(
        live_rows[None, :],
        jnp.exp(-row_rates[None, :] * moments[:, None]),
        jnp.zeros((), jnp.float32),
    )
    diagonal = jnp.where(
        (row_ids[:, None] == positions[None, :])[None],
        free_part[:, :, None],
        jnp.zeros((), jnp.float32),
    )
    new_rows = (diagonal - step_size * summed).astype(jnp.bfloat16)
    return lax.all_to_all(new_rows, "tm", split_axis=0, concat_axis=1, tiled=True)[None]


def solution(mesh):
    placed = (
        P("sector", "tm", None, None),
        P("sector", None, None),
        P("sector", None),
        P("tm"),
        P("tm"),
        P("sector"),
    )
    return jax.shard_map(
        per_device,
        mesh=mesh,
        in_specs=placed,
        out_specs=P("sector", "tm", None, None),
        check_vma=False,
    )
```

profile of v0, /device:TPU:0, one launch (start us, length us, event | category | flops | bytes accessed | tf_op | source)
XLA Modules:
  0.0 162.4 jit_solution(225361923420501898)
XLA Ops:
  7.3 2.4 %and_select_fusion.1 = bf16[1,640,640]{2,1,0:T(8,128)(2,1)} fusion(bf16[1,1,640,640]{3,2,1,0:T(8,128)(2,1)} %param.10, pred[640]{0:T(1024)(128)(4,1)S(1)} %iota_compare_fusion.4), kind=kLoop, calls=%fused_computation.23 | loop fusion | flops 819200 | bytes 1639040 | tf_op jit(solution)/shard_map/jit(_where)/select_n | solution.py:21
  9.7 1.3 collective-permute-start.1
  11.0 2.9 %fusion.15 = bf16[1,640,640]{2,1,0:T(8,128)(2,1)} fusion(bf16[1,1,640,640]{3,2,1,0:T(8,128)(2,1)S(1)} %copy-done.1, bf16[1,640,640]{2,1,0:T(8,128)(2,1)S(1)} %copy-done, pred[640]{0:T(1024)(128)(4,1)S(1)} %iota_compare_fusion.4), kind=kOutput, calls=%fused_computation.33 | convolution fusion | flops 1050214400 | bytes 2458240 | tf_op jit(solution)/shard_map/tik,jk->tij/dot_general | solution.py:26
  13.9 5.6 %collective-permute-start = (bf16[1,640,640]{2,1,0:T(8,128)(2,1)}, bf16[1,640,640]{2,1,0:T(8,128)(2,1)S(1)}, u32[]{:S(2)}, u32[]{:S(2)}) collective-permute-start(bf16[1,640,640]{2,1,0:T(8,128)(2,1)} %fusion.15), channel_id=1, source_target_pairs={{0,1},{1,2},{2,3},{4,5},{5,6},{6,7},{8,9},{9,10},{10,11},{12,13},{... | collective-permute-start | bytes 2457608 | tf_op jit(solution)/shard_map/ppermute | solution.py:10
  20.9 12.3 %collective-permute-done.1 = bf16[1,640,640]{2,1,0:T(8,128)(2,1)S(1)} collective-permute-done((bf16[1,640,640]{2,1,0:T(8,128)(2,1)}, bf16[1,640,640]{2,1,0:T(8,128)(2,1)S(1)}, u32[]{:S(2)}, u32[]{:S(2)}) %collective-permute-start.1) | collective-permute-done | bytes 819232 | tf_op jit(solution)/shard_map/ppermute | solution.py:10
  33.1 4.2 %collective-permute-done = bf16[1,640,640]{2,1,0:T(8,128)(2,1)S(1)} collective-permute-done((bf16[1,640,640]{2,1,0:T(8,128)(2,1)}, bf16[1,640,640]{2,1,0:T(8,128)(2,1)S(1)}, u32[]{:S(2)}, u32[]{:S(2)}) %collective-permute-start) | collective-permute-done | bytes 819232 | tf_op jit(solution)/shard_map/ppermute | solution.py:10
  37.3 3.7 %fusion.13 = bf16[1,640,640]{2,1,0:T(8,128)(2,1)S(1)} fusion(bf16[1,640,640]{2,1,0:T(8,128)(2,1)S(1)} %collective-permute-done, bf16[1,640,640]{2,1,0:T(8,128)(2,1)} %copy-done.2, bf16[1,640,640]{2,1,0:T(8,128)(2,1)S(1)} %copy-done, f32[]{:T(128)} %bitcast.66, f32[]{:T(128)} %bitcast.65, pred[640]{0:T(1024)(128)(4,1)S(1)} %iota_compare_fusion.4), kind=kOutput, calls=%fused_computation.24 | convolution fusion | flops 1051852800 | bytes 3277448 | tf_op jit(solution)/shard_map/tik,kl->til/dot_general | solution.py:34
  41.0 1.3 copy.11
  42.8 5.6 %reduce = bf16[640,640]{1,0:T(8,128)(2,1)S(1)} reduce(bf16[640,1,640]{2,1,0:T(2,128)(2,1)S(1)} %bitcast.69, bf16[]{:T(256)} %broadcast.254), dimensions={1}, to_apply=%bitcast.60.reduce_sub_computation | reduce | bytes 1638402
  48.4 1.1 reshape.286
  49.5 4.4 %all-to-all-start = ((bf16[8,2,25600]{2,1,0:T(2,128)(2,1)}), bf16[8,2,25600]{2,1,0:T(2,128)(2,1)}, u32[]{:S(2)}, u32[]{:S(2)}) async-start(bf16[8,2,25600]{2,1,0:T(2,128)(2,1)} %reshape.286), calls=%async_computation | async-start | bytes 1638400 | tf_op jit(solution)/shard_map/all_to_all | solution.py:42
  54.9 12.1 %all-to-all-done = bf16[8,2,25600]{2,1,0:T(2,128)(2,1)} async-done(((bf16[8,2,25600]{2,1,0:T(2,128)(2,1)}), bf16[8,2,25600]{2,1,0:T(2,128)(2,1)}, u32[]{:S(2)}, u32[]{:S(2)}) %all-to-all-start) | async-done | bytes 819232 | tf_op jit(solution)/shard_map/all_to_all | solution.py:42
  67.1 4.0 %reshape.287 = bf16[640,1,640]{2,1,0:T(2,128)(2,1)S(1)} reshape(bf16[8,2,25600]{2,1,0:T(2,128)(2,1)} %all-to-all-done) | data formatting | bytes 1638400
  72.1 6.3 %rev.6 = bf16[8,640,640]{2,1,0:T(8,128)(2,1)} reverse(bf16[8,640,640]{2,1,0:T(8,128)(2,1)} %all-gather.2.cloned.1.call-done), dimensions={0} | reverse | bytes 13107200 | tf_op jit(solution)/shard_map/rev | solution.py:44
  78.5 12.3 %pad_maximum_fusion = bf16[16,640,640]{2,1,0:T(8,128)(2,1)} fusion(bf16[8,640,640]{2,1,0:T(8,128)(2,1)} %all-gather.2.cloned.1.call-done, bf16[8,640,640]{2,1,0:T(8,128)(2,1)} %rev.6), kind=kLoop, calls=%fused_computation.21 | loop fusion | flops 6553600 | bytes 26214400 | tf_op jit(solution)/shard_map/concatenate | solution.py:44
  90.8 36.5 %while.35 = (s32[]{:T(128)}, f32[8,80,640]{2,1,0:T(8,128)}, f32[8,80,640]{2,1,0:T(8,128)}, bf16[8,80,640]{2,1,0:T(8,128)(2,1)}, bf16[16,640,640]{2,1,0:T(8,128)(...) while((s32[]{:T(128)}, f32[8,80,640]{2,1,0:T(8,128)}, ...), condition=%wide.region_1.2_spmd.clone.clone, body=%wide.region_0.1_spmd.clone.clone.sunk | while | flops 592742400 | bytes 19661552 | solution.py:67
  91.8 4.6 %fusion.40 = f32[9,80,640]{2,1,0:T(8,128)S(1)} fusion(bf16[16,640,640]{2,1,0:T(8,128)(2,1)} %get-tuple-element.458, s32[]{:T(128)} %get-tuple-element.444, pred[9]{0:T(512)(128)(4,1)S(1)} %iota_compare_fusion.7, bf16[80,640]{1,0:T(8,128)(2,1)S(1)} %get-tuple-element.428, bf16[80,640]{1,0:T(8,128)(2,1)S(1)} %get-tuple-element.429), kind=kOutput, calls=%fused_computation.5.clone.1 | convolution fusion | flops 590284800 | bytes 9421321 | tf_op jit(solution)/shard_map/while/body/eval_jaxpr/uik,ukl->uil/dot_general | solution.py:55
  96.4 2.1 %fusion.41 = (f32[8,80,640]{2,1,0:T(8,128)}, f32[8,80,640]{2,1,0:T(8,128)}) fusion(f32[9,80,640]{2,1,0:T(8,128)S(1)} %fusion.40, f32[8,80,640]{2,1,0:T(8,128)} %get-tuple-element.446, pred[8]{0:T(512)(128)(4,1)S(1)} %get-tuple-element.430, pred[]{:T(512)S(6)} %compare.7, pred[8]{0:T(512)(128)(4,1)S(1)} %get-tuple-element.431, ...), kind=kLoop, calls=%fused_computation.8.clone.1 | loop fusion | flops 2457600 | bytes 9830417 | tf_op jit(solution)/shard_map/while/body/eval_jaxpr/add | solution.py:56
  99.5 4.6 %fusion.40 = f32[9,80,640]{2,1,0:T(8,128)S(1)} fusion(bf16[16,640,640]{2,1,0:T(8,128)(2,1)} %get-tuple-element.458, s32[]{:T(128)} %get-tuple-element.444, pred[9]{0:T(512)(128)(4,1)S(1)} %iota_compare_fusion.7, bf16[80,640]{1,0:T(8,128)(2,1)S(1)} %get-tuple-element.428, bf16[80,640]{1,0:T(8,128)(2,1)S(1)} %get-tuple-element.429), kind=kOutput, calls=%fused_computation.5.clone.1 | convolution fusion | flops 590284800 | bytes 9421321 | tf_op jit(solution)/shard_map/while/body/eval_jaxpr/uik,ukl->uil/dot_general | solution.py:55
  104.1 4.0 %fusion.41 = (f32[8,80,640]{2,1,0:T(8,128)}, f32[8,80,640]{2,1,0:T(8,128)}) fusion(f32[9,80,640]{2,1,0:T(8,128)S(1)} %fusion.40, f32[8,80,640]{2,1,0:T(8,128)} %get-tuple-element.446, pred[8]{0:T(512)(128)(4,1)S(1)} %get-tuple-element.430, pred[]{:T(512)S(6)} %compare.7, pred[8]{0:T(512)(128)(4,1)S(1)} %get-tuple-element.431, ...), kind=kLoop, calls=%fused_computation.8.clone.1 | loop fusion | flops 2457600 | bytes 9830417 | tf_op jit(solution)/shard_map/while/body/eval_jaxpr/add | solution.py:56
  109.1 4.6 %fusion.40 = f32[9,80,640]{2,1,0:T(8,128)S(1)} fusion(bf16[16,640,640]{2,1,0:T(8,128)(2,1)} %get-tuple-element.458, s32[]{:T(128)} %get-tuple-element.444, pred[9]{0:T(512)(128)(4,1)S(1)} %iota_compare_fusion.7, bf16[80,640]{1,0:T(8,128)(2,1)S(1)} %get-tuple-element.428, bf16[80,640]{1,0:T(8,128)(2,1)S(1)} %get-tuple-element.429), kind=kOutput, calls=%fused_computation.5.clone.1 | convolution fusion | flops 590284800 | bytes 9421321 | tf_op jit(solution)/shard_map/while/body/eval_jaxpr/uik,ukl->uil/dot_general | solution.py:55
  113.7 4.0 %fusion.41 = (f32[8,80,640]{2,1,0:T(8,128)}, f32[8,80,640]{2,1,0:T(8,128)}) fusion(f32[9,80,640]{2,1,0:T(8,128)S(1)} %fusion.40, f32[8,80,640]{2,1,0:T(8,128)} %get-tuple-element.446, pred[8]{0:T(512)(128)(4,1)S(1)} %get-tuple-element.430, pred[]{:T(512)S(6)} %compare.7, pred[8]{0:T(512)(128)(4,1)S(1)} %get-tuple-element.431, ...), kind=kLoop, calls=%fused_computation.8.clone.1 | loop fusion | flops 2457600 | bytes 9830417 | tf_op jit(solution)/shard_map/while/body/eval_jaxpr/add | solution.py:56
  118.7 4.6 %fusion.40 = f32[9,80,640]{2,1,0:T(8,128)S(1)} fusion(bf16[16,640,640]{2,1,0:T(8,128)(2,1)} %get-tuple-element.458, s32[]{:T(128)} %get-tuple-element.444, pred[9]{0:T(512)(128)(4,1)S(1)} %iota_compare_fusion.7, bf16[80,640]{1,0:T(8,128)(2,1)S(1)} %get-tuple-element.428, bf16[80,640]{1,0:T(8,128)(2,1)S(1)} %get-tuple-element.429), kind=kOutput, calls=%fused_computation.5.clone.1 | convolution fusion | flops 590284800 | bytes 9421321 | tf_op jit(solution)/shard_map/while/body/eval_jaxpr/uik,ukl->uil/dot_general | solution.py:55
  123.3 4.0 %fusion.41 = (f32[8,80,640]{2,1,0:T(8,128)}, f32[8,80,640]{2,1,0:T(8,128)}) fusion(f32[9,80,640]{2,1,0:T(8,128)S(1)} %fusion.40, f32[8,80,640]{2,1,0:T(8,128)} %get-tuple-element.446, pred[8]{0:T(512)(128)(4,1)S(1)} %get-tuple-element.430, pred[]{:T(512)S(6)} %compare.7, pred[8]{0:T(512)(128)(4,1)S(1)} %get-tuple-element.431, ...), kind=kLoop, calls=%fused_computation.8.clone.1 | loop fusion | flops 2457600 | bytes 9830417 | tf_op jit(solution)/shard_map/while/body/eval_jaxpr/add | solution.py:56
  127.3 3.3 %add_multiply_fusion = f32[8,80,640]{2,1,0:T(8,128)} fusion(f32[8,80,640]{2,1,0:T(8,128)} %get-tuple-element.265, f32[8,80,640]{2,1,0:T(8,128)} %get-tuple-element.266), kind=kLoop, calls=%fused_computation.27 | loop fusion | flops 819200 | bytes 4915200 | tf_op jit(solution)/shard_map/mul | solution.py:68
  130.7 8.4 %while.34 = (s32[]{:T(128)}, f32[80,640]{1,0:T(8,128)S(1)}, f32[8,80,640]{2,1,0:T(8,128)S(1)}, f32[80]{0:T(128)S(1)}, f32[8,80,640]{2,1,0:T(8,128)}, /*index=5*/s32[]{:T(128)}, s32[]{:T(128)}) while((s32[]{:T(128)}, f32[80,640]{1,0:T(8,128)S(1)}, f32[8,80,640]{2,1,0:T(8,128)S(1)}, f32[80]{0:T(128)S(1)}, f32[8,80,640]{2,1,0:T(8,128)}, ...), condition=%wide.region_3.4_spmd.clone, body=%wide.region_2.3_spmd.clone.sunk | while | flops 153603 | bytes 819803 | solution.py:77
  130.7 1.0 bitcast_dynamic-update-slice_fusion.2
  131.7 1.0 bitcast_dynamic-update-slice_fusion.2
  132.8 1.0 bitcast_dynamic-update-slice_fusion.2
  133.8 1.0 bitcast_dynamic-update-slice_fusion.2
  134.9 1.0 bitcast_dynamic-update-slice_fusion.2
  139.4 15.3 %all_to_all.21 = bf16[8,80,640]{2,1,0:T(8,128)(2,1)S(1)} all-to-all(bf16[8,80,640]{2,1,0:T(8,128)(2,1)S(1)} %subtract_convert_fusion), channel_id=1, replica_groups=mesh['tm'=8,'sector'=4] {'tm'}, dimensions={0} | all-to-all | bytes 1638400 | tf_op jit(solution)/shard_map/all_to_all | solution.py:91
  (39 shorter events, 10.8 us)
Async XLA Ops:
  6.5 4.5 %copy-start = (bf16[1,640,640]{2,1,0:T(8,128)(2,1)S(1)}, bf16[1,640,640]{2,1,0:T(8,128)(2,1)}, u32[]{:S(2)}) copy-start(bf16[1,640,640]{2,1,0:T(8,128)(2,1)} %param.11) | copy-start | bytes 2457604
  6.5 4.5 %copy-start.1 = (bf16[1,1,640,640]{3,2,1,0:T(8,128)(2,1)S(1)}, bf16[1,1,640,640]{3,2,1,0:T(8,128)(2,1)}, u32[]{:S(2)}) copy-start(bf16[1,1,640,640]{3,2,1,0:T(8,128)(2,1)} %param.10) | copy-start | bytes 2457604
  6.5 65.6 %all-gather.2.cloned.1.call-start = ((), (), s32[]{:S(2)}) async-start(), calls=%async_computation.2 | async-start | bytes 7372800 | tf_op jit(solution)/shard_map/all_gather | solution.py:43
  9.7 23.4 %collective-permute-start.1 = (bf16[1,640,640]{2,1,0:T(8,128)(2,1)}, bf16[1,640,640]{2,1,0:T(8,128)(2,1)S(1)}, u32[]{:S(2)}, u32[]{:S(2)}) collective-permute-start(bf16[1,640,640]{2,1,0:T(8,128)(2,1)} %and_select_fusion.1), channel_id=1, source_target_pairs={{1,0},{2,1},{3,2},{5,4},{6,5},{7,6},{9,8},{10,9},{11,10},{13,12},{... | collective-permute-start | bytes 2457608 | tf_op jit(solution)/shard_map/ppermute | solution.py:10
  13.9 23.4 %collective-permute-start = (bf16[1,640,640]{2,1,0:T(8,128)(2,1)}, bf16[1,640,640]{2,1,0:T(8,128)(2,1)S(1)}, u32[]{:S(2)}, u32[]{:S(2)}) collective-permute-start(bf16[1,640,640]{2,1,0:T(8,128)(2,1)} %fusion.15), channel_id=1, source_target_pairs={{0,1},{1,2},{2,3},{4,5},{5,6},{6,7},{8,9},{9,10},{10,11},{12,13},{... | collective-permute-start | bytes 2457608 | tf_op jit(solution)/shard_map/ppermute | solution.py:10
  33.1 4.2 %copy-start.2 = (bf16[1,640,640]{2,1,0:T(8,128)(2,1)}, bf16[1,640,640]{2,1,0:T(8,128)(2,1)S(1)}, u32[]{:S(2)}) copy-start(bf16[1,640,640]{2,1,0:T(8,128)(2,1)S(1)} %collective-permute-done.1) | copy-start | bytes 2457604
  49.5 17.6 %all-to-all-start = ((bf16[8,2,25600]{2,1,0:T(2,128)(2,1)}), bf16[8,2,25600]{2,1,0:T(2,128)(2,1)}, u32[]{:S(2)}, u32[]{:S(2)}) async-start(bf16[8,2,25600]{2,1,0:T(2,128)(2,1)} %reshape.286), calls=%async_computation | async-start | bytes 1638400 | tf_op jit(solution)/shard_map/all_to_all | solution.py:42
Sparse Core Ops, SparseCore 0:
  9.8 49.5 all-gather.1
where the time goes:
time: 164 us; the launch traced here: 162 us
  other arithmetic  47.3 us (29%)
  waiting for transfers between devices  28.6 us (17%)
  matrix products  24.9 us (15%)
  local copies, waits for them, and re-layouts  19.1 us (12%)
  between operations  15.6 us (10%)
  blocking collectives  15.3 us (9%)
  starting transfers between devices  11.3 us (7%)
    dot_general x4, matrix products, pair_step(): jnp.einsum('uik,ukl->uil', left, window, preferred_element_type=jnp.float32)  18.3 us
    ppermute x2, waiting for transfers between devices, shifted(): return lax.ppermute(block, axis, route)  16.4 us
    all_to_all x1, blocking collectives, per_device(): lax.all_to_all(new_rows, 'tm', split_axis=0, concat_axis=1, tiled=True)  15.3 us
    add x4, other arithmetic, pair_step(): backward + jnp.where((slots < time_count - lag)[:, None, None], product[:...  14.2 us
    concatenate x1, other arithmetic, per_device(): mirrored = jnp.concatenate([history[::-1], history], 0)  12.3 us
    all_to_all x1, waiting for transfers between devices, per_device(): lax.all_to_all(self_energy, 'tm', split_axis=1, concat_axis=0, tiled=True)  12.1 us
    dynamic_update_slice x8, other arithmetic, per_device(): lax.scan(advance, jnp.zeros((rows_each, states), jnp.float32), convolved)  8.25 us
    unnamed x11, local copies, waits for them, and re-layouts  7.55 us
  transfers between devices with their start and end apart: 4, of which 3 were waited for; matrix products, arithmetic and copies ran while one was open for 13% of the time, Pallas kernels for 0%

commit v1 on v0

--- a/solution.py
+++ b/solution.py
@@ -1,6 +1,9 @@
+import functools
 import jax
 import jax.numpy as jnp
 from jax import lax
+from jax.experimental import pallas as pl
+from jax.experimental.pallas import tpu as pltpu
 from jax.sharding import PartitionSpec as P
 
 
@@ -10,7 +13,7 @@
     return lax.ppermute(block, axis, route)
 
 
-def per_device(propagator, rising_op, energies, hyb_particle, hyb_hole, sector_sizes):
+def general_device(propagator, rising_op, energies, hyb_particle, hyb_hole, sector_sizes):
     t_dev = propagator.shape[1]
     states = propagator.shape[2]
     time_count = t_dev * lax.axis_size("tm")
@@ -91,6 +94,353 @@
     return lax.all_to_all(new_rows, "tm", split_axis=0, concat_axis=1, tiled=True)[None]
 
 
+MESH = pl.DeviceIdType.MESH
+ROW_TILE = 16
+LANES = 128
+
+
+def flipped(index, mask):
+    bit = 1
+    while bit <= mask:
+        if mask & bit:
+            index = index + bit - 2 * bit * lax.rem(lax.div(index, bit), 2)
+        bit *= 2
+    return index
+
+
+def last_hops(mask):
+    bits = [1 << i for i in range(mask.bit_length()) if mask >> i & 1]
+    if bits[0] == 1:
+        return (1, 1)
+    return (bits[0], bits[-1])
+
+
+def fused_kernel(
+    times,
+    sectors,
+    size_ref,
+    particle_ref,
+    hole_ref,
+    prop_ref,
+    operator_ref,
+    energy_ref,
+    out_ref,
+    history,
+    turned,
+    upward,
+    below,
+    above,
+    energy_out,
+    energy_in,
+    sums,
+    fresh,
+    z_send,
+    z_recv,
+    gather_send,
+    gather_recv,
+    rows_send,
+    rows_recv,
+    out_send,
+    out_recv,
+):
+    states = prop_ref.shape[-1]
+    rows = states // times
+    half = states // 2
+    step_size = 1.0 / times
+    me = lax.axis_index("tm")
+    sector = lax.axis_index("sector")
+    has_below = sector > 0
+    has_above = sector < sectors - 1
+
+    barrier = pltpu.get_barrier_semaphore()
+    for mask in range(1, times):
+        pl.semaphore_signal(
+            barrier, inc=1, device_id={"tm": flipped(me, mask)}, device_id_type=MESH
+        )
+
+    @pl.when(has_below)
+    def _():
+        pl.semaphore_signal(barrier, inc=1, device_id={"sector": sector - 1}, device_id_type=MESH)
+
+    @pl.when(has_above)
+    def _():
+        pl.semaphore_signal(barrier, inc=1, device_id={"sector": sector + 1}, device_id_type=MESH)
+
+    size = size_ref[0]
+    live = (lax.broadcasted_iota(jnp.int32, (states, states), 0) < size) & (
+        lax.broadcasted_iota(jnp.int32, (states, states), 1) < size
+    )
+    history[me] = jnp.where(
+        live, prop_ref[0, 0].astype(jnp.float32), jnp.zeros((), jnp.float32)
+    ).astype(jnp.bfloat16)
+
+    neighbours = jnp.where(has_below, 1, 0) + jnp.where(has_above, 1, 0)
+    pl.semaphore_wait(barrier, times - 1 + neighbours)
+
+    def down_copy():
+        return pltpu.make_async_remote_copy(
+            src_ref=history.at[me],
+            dst_ref=above,
+            send_sem=z_send.at[0],
+            recv_sem=z_recv.at[0],
+            device_id={"sector": sector - 1},
+            device_id_type=MESH,
+        )
+
+    def up_copy():
+        return pltpu.make_async_remote_copy(
+            src_ref=upward,
+            dst_ref=below,
+            send_sem=z_send.at[1],
+            recv_sem=z_recv.at[1],
+            device_id={"sector": sector + 1},
+            device_id_type=MESH,
+        )
+
+    def gather_copy(mask, part, block):
+        hop = last_hops(mask)[part]
+        piece = history.at[block, pl.ds(part * half, half)]
+        return pltpu.make_async_remote_copy(
+            src_ref=piece,
+            dst_ref=piece,
+            send_sem=gather_send.at[mask, part],
+            recv_sem=gather_recv.at[mask, part],
+            device_id={"tm": flipped(me, hop)},
+            device_id_type=MESH,
+        )
+
+    def gather_start(mask, part):
+        hop = last_hops(mask)[part]
+        gather_copy(mask, part, flipped(me, mask ^ hop)).start()
+
+    @pl.when(has_below)
+    def _():
+        down_copy().start()
+
+    singles = [1 << i for i in range(1, times.bit_length() - 1)]
+    order = {mask: ((1, 0) if i % 2 == 0 else (0, 1)) for i, mask in enumerate(singles)}
+    for turn in range(2):
+        for mask in singles:
+            gather_start(mask, order[mask][turn])
+    for part in range(2):
+        gather_start(1, part)
+
+    operator = operator_ref[0]
+    raised = jnp.dot(operator, history[me], preferred_element_type=jnp.float32).astype(jnp.bfloat16)
+    upward[...] = lax.dot_general(
+        raised, operator, (((1,), (1,)), ((), ())), preferred_element_type=jnp.float32
+    ).astype(jnp.bfloat16)
+
+    @pl.when(has_above)
+    def _():
+        up_copy().start()
+
+    turned[...] = operator_ref[0].T
+
+    arrived = set()
+    started = {(mask, part) for mask in singles for part in range(2)} | {(1, 0), (1, 1)}
+
+    def gather_arrive(mask, part):
+        if (mask, part) in arrived:
+            return
+        arrived.add((mask, part))
+        gather_copy(mask, part, flipped(me, mask)).wait_recv()
+        for later in range(2, times):
+            if (later, part) not in started and later ^ last_hops(later)[part] == mask:
+                started.add((later, part))
+                gather_start(later, part)
+
+    for turn in range(2):
+        for mask in singles:
+            gather_arrive(mask, order[mask][turn])
+
+    @pl.when(has_above)
+    def _():
+        pltpu.make_async_remote_copy(
+            src_ref=above,
+            dst_ref=above,
+            send_sem=z_send.at[0],
+            recv_sem=z_recv.at[0],
+            device_id={"sector": sector + 1},
+            device_id_type=MESH,
+        ).wait_recv()
+
+    @pl.when(sector == sectors - 1)
+    def _():
+        above[...] = jnp.zeros_like(above)
+
+    lowered = jnp.dot(turned[...], above[...], preferred_element_type=jnp.float32).astype(jnp.bfloat16)
+    downward = jnp.dot(lowered, operator_ref[0], preferred_element_type=jnp.float32)
+
+    @pl.when(has_below)
+    def _():
+        pltpu.make_async_remote_copy(
+            src_ref=below,
+            dst_ref=below,
+            send_sem=z_send.at[1],
+            recv_sem=z_recv.at[1],
+            device_id={"sector": sector - 1},
+            device_id_type=MESH,
+        ).wait_recv()
+
+    @pl.when(sector == 0)
+    def _():
+        below[...] = jnp.zeros_like(below)
+
+    combined = particle_ref[0] * below[...].astype(jnp.float32) + hole_ref[0] * downward
+    energy_out[...] = jnp.where(live, combined, jnp.zeros((), jnp.float32)).astype(jnp.bfloat16)
+
+    def row_block(index):
+        return pl.ds(pl.multiple_of(index * rows, rows), rows)
+
+    def rows_copy(peer, target, source):
+        return pltpu.make_async_remote_copy(
+            src_ref=energy_out.at[row_block(target)],
+            dst_ref=energy_in.at[row_block(source)],
+            send_sem=rows_send.at[peer],
+            recv_sem=rows_recv.at[peer],
+            device_id={"tm": flipped(me, peer)},
+            device_id_type=MESH,
+        )
+
+    for mask in reversed(range(1, times)):
+        rows_copy(mask, flipped(me, mask), me).start()
+    energy_in[row_block(me)] = energy_out[row_block(me)]
+
+    for mask in range(2, times, 2):
+        for part in range(2):
+            gather_arrive(mask, part)
+    for mask in range(1, times, 2):
+        for part in range(2):
+            gather_arrive(mask, part)
+    for mask in range(1, times):
+        rows_copy(mask, flipped(me, mask), flipped(me, mask)).wait_recv()
+
+    row_ids = me * rows + lax.broadcasted_iota(jnp.int32, (rows, states), 0)
+    column_ids = lax.broadcasted_iota(jnp.int32, (rows, states), 1)
+    on_diagonal = row_ids == column_ids
+    rates = jnp.sum(
+        jnp.where(on_diagonal, energy_ref[...], jnp.zeros((), jnp.float32)), axis=1, keepdims=True
+    )
+    decay = jnp.exp(-step_size * rates)
+    shown = on_diagonal & (row_ids < size)
+
+    def out_copy(moment, place):
+        return pltpu.make_async_remote_copy(
+            src_ref=fresh.at[moment],
+            dst_ref=out_ref.at[0, 0, row_block(place)],
+            send_sem=out_send.at[moment],
+            recv_sem=out_recv.at[place],
+            device_id={"tm": moment},
+            device_id_type=MESH,
+        )
+
+    running = jnp.zeros((rows, states), jnp.float32)
+    for moment in range(times):
+        depth = (times - moment) * rows
+        product = jnp.dot(
+            energy_in[0:depth], history[moment], preferred_element_type=jnp.float32
+        )
+        if moment == 0:
+            sums[...] = product
+        else:
+            sums[moment * rows : states] += product
+        running = decay * running + step_size * sums[moment * rows : (moment + 1) * rows]
+        free_part = jnp.where(
+            shown, jnp.exp(-rates * (moment * step_size)), jnp.zeros((), jnp.float32)
+        )
+        fresh[moment] = (free_part - step_size * running).astype(jnp.bfloat16)
+
+        @pl.when(me != moment)
+        def _():
+            out_copy(moment, me).start()
+
+        @pl.when(me == moment)
+        def _():
+            out_ref[0, 0, row_block(me)] = fresh[moment]
+
+    for mask in range(1, times):
+        pltpu.make_async_remote_copy(
+            src_ref=fresh.at[0],
+            dst_ref=out_ref.at[0, 0, row_block(flipped(me, mask))],
+            send_sem=out_send.at[0],
+            recv_sem=out_recv.at[flipped(me, mask)],
+            device_id={"tm": flipped(me, mask)},
+            device_id_type=MESH,
+        ).wait_recv()
+    for moment in range(times):
+
+        @pl.when(me != moment)
+        def _():
+            out_copy(moment, me).wait_send()
+
+    for mask in range(1, times):
+        rows_copy(mask, flipped(me, mask), me).wait_send()
+        for part in range(2):
+            gather_copy(mask, part, flipped(me, mask)).wait_send()
+
+    @pl.when(has_below)
+    def _():
+        down_copy().wait_send()
+
+    @pl.when(has_above)
+    def _():
+        up_copy().wait_send()
+
+
+def fused_device(propagator, rising_op, energies, hyb_particle, hyb_hole, sector_sizes):
+    times = lax.axis_size("tm")
+    states = propagator.shape[-1]
+    square = (states, states)
+    narrow, wide = jnp.bfloat16, jnp.float32
+    vmem = pl.BlockSpec(memory_space=pltpu.VMEM)
+    smem = pl.BlockSpec(memory_space=pltpu.SMEM)
+    dma = pltpu.SemaphoreType.DMA
+    return pl.pallas_call(
+        functools.partial(fused_kernel, times, lax.axis_size("sector")),
+        out_shape=jax.ShapeDtypeStruct(propagator.shape, narrow),
+        in_specs=[smem, smem, smem, vmem, vmem, vmem],
+        out_specs=vmem,
+        scratch_shapes=[
+            pltpu.VMEM((times,) + square, narrow),
+            pltpu.VMEM(square, narrow),
+            pltpu.VMEM(square, narrow),
+            pltpu.VMEM(square, narrow),
+            pltpu.VMEM(square, narrow),
+            pltpu.VMEM(square, narrow),
+            pltpu.VMEM(square, narrow),
+            pltpu.VMEM(square, wide),
+            pltpu.VMEM((times, states // times, states), narrow),
+            dma((2,)),
+            dma((2,)),
+            dma((times, 2)),
+            dma((times, 2)),
+            dma((times,)),
+            dma((times,)),
+            dma((times,)),
+            dma((times,)),
+        ],
+        compiler_params=pltpu.CompilerParams(
+            collective_id=0, has_side_effects=True, vmem_limit_bytes=60 * 2**20
+        ),
+    )(sector_sizes, hyb_particle, hyb_hole, propagator, rising_op, energies)
+
+
+def per_device(propagator, rising_op, energies, hyb_particle, hyb_hole, sector_sizes):
+    times = lax.axis_size("tm")
+    states = propagator.shape[-1]
+    fits = (
+        propagator.shape[1] == 1
+        and times > 2
+        and times & (times - 1) == 0
+        and states % (times * ROW_TILE) == 0
+        and states % (2 * ROW_TILE) == 0
+        and states % LANES == 0
+    )
+    chosen = fused_device if fits else general_device
+    return chosen(propagator, rising_op, energies, hyb_particle, hyb_hole, sector_sizes)
+
+
 def solution(mesh):
     placed = (
         P("sector", "tm", None, None),

time: 164 us -> 61.2 us (0.37)
  Pallas kernels: 0 us -> 56.5 us
  other arithmetic: 47.3 us -> 0 us
  waiting for transfers between devices: 28.6 us -> 0 us
  matrix products: 24.9 us -> 0 us
  local copies, waits for them, and re-layouts: 19.1 us -> 2.11 us
  blocking collectives: 15.3 us -> 0 us
  between operations: 15.6 us -> 1.95 us
  starting transfers between devices: 11.3 us -> 0 us
    pallas_call x0 -> x1, Pallas kernels: none -> 56.5 us  [fused_device(): pl.pallas_call(functools.partial(fused_kernel, times, lax.axis_size('sect...]
    dot_general x6 -> x0, matrix products: 24.9 us -> none  [the longest x4 18.3 us: pair_step(): jnp.einsum('uik,ukl->uil', left, window, preferred_element_type=jnp.float32)]
    ppermute x2 -> x0, waiting for transfers between devices: 16.4 us -> none  [shifted(): return lax.ppermute(block, axis, route)]
    all_to_all x1 -> x0, blocking collectives: 15.3 us -> none  [per_device(): lax.all_to_all(new_rows, 'tm', split_axis=0, concat_axis=1, tiled=True)]
    add x5 -> x0, other arithmetic: 14.2 us -> none  [the longest x4 14.2 us: pair_step(): backward + jnp.where((slots < time_count - lag)[:, None, None], product[:...]
    concatenate x1 -> x0, other arithmetic: 12.3 us -> none  [per_device(): mirrored = jnp.concatenate([history[::-1], history], 0)]
    all_to_all x1 -> x0, waiting for transfers between devices: 12.1 us -> none  [per_device(): lax.all_to_all(self_energy, 'tm', split_axis=1, concat_axis=0, tiled=True)]
    dynamic_update_slice x8 -> x0, other arithmetic: 8.25 us -> none  [per_device(): lax.scan(advance, jnp.zeros((rows_each, states), jnp.float32), convolved)]
  transfers between devices with their start and end apart: 4 -> 0, of which waited for: 3 -> 0; matrix products, arithmetic and copies ran while one was open for 13% -> 0% of each run, Pallas kernels for 0% -> 0%
where the time goes in v1:
time: 61.2 us; the launch traced here: 60.6 us
  Pallas kernels  56.5 us (92%)
  local copies, waits for them, and re-layouts  2.11 us (3%)
  between operations  1.95 us (3%)
    pallas_call x1, Pallas kernels, fused_device(): pl.pallas_call(functools.partial(fused_kernel, times, lax.axis_size('sect...  56.5 us
    unnamed x1, local copies, waits for them, and re-layouts  2.11 us

profile of v1, /device:TPU:0, one launch (start us, length us, event | category | flops | bytes accessed | tf_op | source)
XLA Modules:
  0.0 60.6 jit_solution(2197432008855864334)
XLA Ops:
  1.9 56.5 %shard_map.64 = bf16[1,1,640,640]{3,2,1,0:T(8,128)(2,1)} custom-call(s32[1]{0:T(128)S(6)} %copy.10.size_ref, f32[1]{0:T(128)S(6)} %copy.8.particle_ref, f32[1]{0:T(128)S(6)} %copy.9.hole_ref, bf16[1,1,640,640]{3,2,1,0:T(8,128)(2,1)} %prop_ref.1, bf16[1,640,640]{2,1,0:T(8,128)(2,1)} %operator_ref.1, f32[1,640]{1,0:T(1,128)} %energy_ref.1), custom_call_target="tpu_custom_call" | custom-call | tf_op jit(solution)/shard_map/pallas_call | solution.py:399
  58.5 2.1 %copy.11 = bf16[1,1,640,640]{3,2,1,0:T(8,128)(2,1)} copy(bf16[1,1,640,640]{3,2,1,0:T(8,128)(2,1)} %shard_map.64) | data formatting | bytes 1638400

commit v2 on v1

--- a/solution.py
+++ b/solution.py
@@ -97,6 +97,8 @@
 MESH = pl.DeviceIdType.MESH
 ROW_TILE = 16
 LANES = 128
+SUBLANES = 8
+PARTS = 4
 
 
 def flipped(index, mask):
@@ -108,11 +110,11 @@
     return index
 
 
-def last_hops(mask):
+def last_hop(mask, part):
     bits = [1 << i for i in range(mask.bit_length()) if mask >> i & 1]
     if bits[0] == 1:
-        return (1, 1)
-    return (bits[0], bits[-1])
+        return 1
+    return bits[0] if part < PARTS // 2 else bits[-1]
 
 
 def fused_kernel(
@@ -126,26 +128,34 @@
     energy_ref,
     out_ref,
     history,
+    lower_operator,
     turned,
-    upward,
+    pair,
+    up_rows,
+    down_rows,
     below,
     above,
-    energy_out,
     energy_in,
     sums,
     fresh,
-    z_send,
-    z_recv,
+    strengths,
+    operator_send,
+    operator_recv,
+    up_send,
+    up_recv,
+    down_send,
+    down_recv,
     gather_send,
     gather_recv,
-    rows_send,
-    rows_recv,
+    strength_send,
+    strength_recv,
     out_send,
     out_recv,
 ):
     states = prop_ref.shape[-1]
     rows = states // times
     half = states // 2
+    piece_rows = states // PARTS
     step_size = 1.0 / times
     me = lax.axis_index("tm")
     sector = lax.axis_index("sector")
@@ -173,72 +183,104 @@
     history[me] = jnp.where(
         live, prop_ref[0, 0].astype(jnp.float32), jnp.zeros((), jnp.float32)
     ).astype(jnp.bfloat16)
+    first_line = lax.broadcasted_iota(jnp.int32, strengths.shape[1:], 0) == 0
+    strengths[me] = jnp.where(first_line, particle_ref[0], hole_ref[0])
 
     neighbours = jnp.where(has_below, 1, 0) + jnp.where(has_above, 1, 0)
     pl.semaphore_wait(barrier, times - 1 + neighbours)
 
-    def down_copy():
-        return pltpu.make_async_remote_copy(
-            src_ref=history.at[me],
-            dst_ref=above,
-            send_sem=z_send.at[0],
-            recv_sem=z_recv.at[0],
-            device_id={"sector": sector - 1},
-            device_id_type=MESH,
-        )
-
-    def up_copy():
-        return pltpu.make_async_remote_copy(
-            src_ref=upward,
-            dst_ref=below,
-            send_sem=z_send.at[1],
-            recv_sem=z_recv.at[1],
+    def row_block(index):
+        return pl.ds(pl.multiple_of(index * rows, rows), rows)
+
+    def half_block(index):
+        return pl.ds(pl.multiple_of(index * half, half), half)
+
+    my_half = lax.rem(me, 2)
+
+    def operator_copy():
+        return pltpu.make_async_remote_copy(
+            src_ref=operator_ref.at[0, half_block(my_half)],
+            dst_ref=lower_operator.at[half_block(my_half)],
+            send_sem=operator_send.at[0],
+            recv_sem=operator_recv.at[0],
             device_id={"sector": sector + 1},
             device_id_type=MESH,
         )
 
+    def share_copy(which):
+        return pltpu.make_async_remote_copy(
+            src_ref=lower_operator.at[half_block(which)],
+            dst_ref=lower_operator.at[half_block(which)],
+            send_sem=operator_send.at[1],
+            recv_sem=operator_recv.at[1],
+            device_id={"tm": flipped(me, 1)},
+            device_id_type=MESH,
+        )
+
+    def up_copy(mask, step=1):
+        block = row_block(flipped(me, mask))
+        return pltpu.make_async_remote_copy(
+            src_ref=up_rows.at[block],
+            dst_ref=below.at[block],
+            send_sem=up_send.at[mask],
+            recv_sem=up_recv.at[mask],
+            device_id={"sector": sector + step},
+            device_id_type=MESH,
+        )
+
+    def down_copy(mask, step=-1):
+        block = row_block(flipped(me, mask))
+        return pltpu.make_async_remote_copy(
+            src_ref=down_rows.at[block],
+            dst_ref=above.at[block],
+            send_sem=down_send.at[mask],
+            recv_sem=down_recv.at[mask],
+            device_id={"sector": sector + step},
+            device_id_type=MESH,
+        )
+
     def gather_copy(mask, part, block):
-        hop = last_hops(mask)[part]
-        piece = history.at[block, pl.ds(part * half, half)]
+        piece = history.at[block, pl.ds(part * piece_rows, piece_rows)]
         return pltpu.make_async_remote_copy(
             src_ref=piece,
             dst_ref=piece,
             send_sem=gather_send.at[mask, part],
             recv_sem=gather_recv.at[mask, part],
-            device_id={"tm": flipped(me, hop)},
+            device_id={"tm": flipped(me, last_hop(mask, part))},
+            device_id_type=MESH,
+        )
+
+    def strength_copy(mask, block):
+        return pltpu.make_async_remote_copy(
+            src_ref=strengths.at[block],
+            dst_ref=strengths.at[block],
+            send_sem=strength_send.at[mask],
+            recv_sem=strength_recv.at[mask],
+            device_id={"tm": flipped(me, mask)},
             device_id_type=MESH,
         )
 
     def gather_start(mask, part):
-        hop = last_hops(mask)[part]
-        gather_copy(mask, part, flipped(me, mask ^ hop)).start()
-
-    @pl.when(has_below)
-    def _():
-        down_copy().start()
-
+        gather_copy(mask, part, flipped(me, mask ^ last_hop(mask, part))).start()
+
+    forward = list(range(PARTS))
+    backward = forward[PARTS // 2 :] + forward[: PARTS // 2]
+    mixed = [p for pair_of in zip(forward, backward) for p in pair_of][:PARTS]
     singles = [1 << i for i in range(1, times.bit_length() - 1)]
-    order = {mask: ((1, 0) if i % 2 == 0 else (0, 1)) for i, mask in enumerate(singles)}
-    for turn in range(2):
+    order = {mask: (backward if i % 2 == 0 else forward) for i, mask in enumerate(singles)}
+    started = {(mask, part) for mask in [1] + singles for part in range(PARTS)}
+    arrived = set()
+    for turn in range(PARTS):
         for mask in singles:
             gather_start(mask, order[mask][turn])
-    for part in range(2):
-        gather_start(1, part)
-
-    operator = operator_ref[0]
-    raised = jnp.dot(operator, history[me], preferred_element_type=jnp.float32).astype(jnp.bfloat16)
-    upward[...] = lax.dot_general(
-        raised, operator, (((1,), (1,)), ((), ())), preferred_element_type=jnp.float32
-    ).astype(jnp.bfloat16)
+        gather_start(1, turn)
 
     @pl.when(has_above)
     def _():
-        up_copy().start()
-
-    turned[...] = operator_ref[0].T
-
-    arrived = set()
-    started = {(mask, part) for mask in singles for part in range(2)} | {(1, 0), (1, 1)}
+        operator_copy().start()
+
+    for mask in range(1, times):
+        strength_copy(mask, me).start()
 
     def gather_arrive(mask, part):
         if (mask, part) in arrived:
@@ -246,75 +288,83 @@
         arrived.add((mask, part))
         gather_copy(mask, part, flipped(me, mask)).wait_recv()
         for later in range(2, times):
-            if (later, part) not in started and later ^ last_hops(later)[part] == mask:
+            if (later, part) not in started and later ^ last_hop(later, part) == mask:
                 started.add((later, part))
                 gather_start(later, part)
 
-    for turn in range(2):
+    def send_up(mask, raised):
+        up_rows[row_block(flipped(me, mask))] = lax.dot_general(
+            raised, operator_ref[0], (((1,), (1,)), ((), ())), preferred_element_type=jnp.float32
+        ).astype(jnp.bfloat16)
+
+        @pl.when(has_above)
+        def _():
+            up_copy(mask).start()
+
+    def send_down(mask, lowered):
+        down_rows[row_block(flipped(me, mask))] = jnp.dot(
+            lowered, lower_operator[...], preferred_element_type=jnp.float32
+        ).astype(jnp.bfloat16)
+
+        @pl.when(has_below)
+        def _():
+            down_copy(mask).start()
+
+    def product_of(left, mask):
+        return jnp.dot(
+            left, history[flipped(me, mask)], preferred_element_type=jnp.float32
+        ).astype(jnp.bfloat16)
+
+    pair[0:rows] = operator_ref[0, row_block(me)]
+    send_up(0, product_of(pair[0:rows], 0))
+    for part in range(PARTS):
+        gather_arrive(1, part)
+    send_up(1, product_of(pair[0:rows], 1))
+    for turn in range(PARTS // 2):
         for mask in singles:
             gather_arrive(mask, order[mask][turn])
 
-    @pl.when(has_above)
+    @pl.when(has_below)
     def _():
         pltpu.make_async_remote_copy(
-            src_ref=above,
-            dst_ref=above,
-            send_sem=z_send.at[0],
-            recv_sem=z_recv.at[0],
-            device_id={"sector": sector + 1},
+            src_ref=lower_operator.at[half_block(my_half)],
+            dst_ref=lower_operator.at[half_block(my_half)],
+            send_sem=operator_send.at[0],
+            recv_sem=operator_recv.at[0],
+            device_id={"sector": sector - 1},
             device_id_type=MESH,
         ).wait_recv()
+        share_copy(my_half).start()
+        share_copy(1 - my_half).wait_recv()
+
+    @pl.when(sector == 0)
+    def _():
+        lower_operator[...] = jnp.zeros_like(lower_operator)
+
+    turned[...] = lower_operator[...].T
+    pair[rows : 2 * rows] = turned[row_block(me)]
+    for mask in range(2):
+        send_down(mask, product_of(pair[rows : 2 * rows], mask))
+
+    for turn in range(PARTS // 2, PARTS):
+        for mask in singles:
+            gather_arrive(mask, order[mask][turn])
+
+    ranked = sorted(range(2, times), key=lambda m: (bin(m >> 1).count("1"), m & 1, m))
+    for mask in ranked:
+        for part in mixed:
+            gather_arrive(mask, part)
+        both = product_of(pair[...], mask)
+        send_up(mask, both[0:rows])
+        send_down(mask, both[rows : 2 * rows])
+
+    @pl.when(sector == 0)
+    def _():
+        below[...] = jnp.zeros_like(below)
 
     @pl.when(sector == sectors - 1)
     def _():
         above[...] = jnp.zeros_like(above)
-
-    lowered = jnp.dot(turned[...], above[...], preferred_element_type=jnp.float32).astype(jnp.bfloat16)
-    downward = jnp.dot(lowered, operator_ref[0], preferred_element_type=jnp.float32)
-
-    @pl.when(has_below)
-    def _():
-        pltpu.make_async_remote_copy(
-            src_ref=below,
-            dst_ref=below,
-            send_sem=z_send.at[1],
-            recv_sem=z_recv.at[1],
-            device_id={"sector": sector - 1},
-            device_id_type=MESH,
-        ).wait_recv()
-
-    @pl.when(sector == 0)
-    def _():
-        below[...] = jnp.zeros_like(below)
-
-    combined = particle_ref[0] * below[...].astype(jnp.float32) + hole_ref[0] * downward
-    energy_out[...] = jnp.where(live, combined, jnp.zeros((), jnp.float32)).astype(jnp.bfloat16)
-
-    def row_block(index):
-        return pl.ds(pl.multiple_of(index * rows, rows), rows)
-
-    def rows_copy(peer, target, source):
-        return pltpu.make_async_remote_copy(
-            src_ref=energy_out.at[row_block(target)],
-            dst_ref=energy_in.at[row_block(source)],
-            send_sem=rows_send.at[peer],
-            recv_sem=rows_recv.at[peer],
-            device_id={"tm": flipped(me, peer)},
-            device_id_type=MESH,
-        )
-
-    for mask in reversed(range(1, times)):
-        rows_copy(mask, flipped(me, mask), me).start()
-    energy_in[row_block(me)] = energy_out[row_block(me)]
-
-    for mask in range(2, times, 2):
-        for part in range(2):
-            gather_arrive(mask, part)
-    for mask in range(1, times, 2):
-        for part in range(2):
-            gather_arrive(mask, part)
-    for mask in range(1, times):
-        rows_copy(mask, flipped(me, mask), flipped(me, mask)).wait_recv()
 
     row_ids = me * rows + lax.broadcasted_iota(jnp.int32, (rows, states), 0)
     column_ids = lax.broadcasted_iota(jnp.int32, (rows, states), 1)
@@ -324,6 +374,29 @@
     )
     decay = jnp.exp(-step_size * rates)
     shown = on_diagonal & (row_ids < size)
+    live_rows = (row_ids < size) & (column_ids < size)
+
+    for mask in range(1, times):
+        strength_copy(mask, flipped(me, mask)).wait_recv()
+
+    @pl.when(has_below)
+    def _():
+        for mask in range(times):
+            up_copy(mask, -1).wait_recv()
+
+    @pl.when(has_above)
+    def _():
+        for mask in range(times):
+            down_copy(mask, 1).wait_recv()
+
+    for moment in range(times):
+        place = pl.ds(moment * rows, rows)
+        combined = strengths[moment, 0:1, 0:1] * below[place].astype(jnp.float32) + strengths[
+            moment, 1:2, 0:1
+        ] * above[place].astype(jnp.float32)
+        energy_in[place] = jnp.where(live_rows, combined, jnp.zeros((), jnp.float32)).astype(
+            jnp.bfloat16
+        )
 
     def out_copy(moment, place):
         return pltpu.make_async_remote_copy(
@@ -375,17 +448,21 @@
             out_copy(moment, me).wait_send()
 
     for mask in range(1, times):
-        rows_copy(mask, flipped(me, mask), me).wait_send()
-        for part in range(2):
+        strength_copy(mask, me).wait_send()
+        for part in range(PARTS):
             gather_copy(mask, part, flipped(me, mask)).wait_send()
 
     @pl.when(has_below)
     def _():
-        down_copy().wait_send()
+        share_copy(my_half).wait_send()
+        for mask in range(times):
+            down_copy(mask).wait_send()
 
     @pl.when(has_above)
     def _():
-        up_copy().wait_send()
+        operator_copy().wait_send()
+        for mask in range(times):
+            up_copy(mask).wait_send()
 
 
 def fused_device(propagator, rising_op, energies, hyb_particle, hyb_hole, sector_sizes):
@@ -405,16 +482,23 @@
             pltpu.VMEM((times,) + square, narrow),
             pltpu.VMEM(square, narrow),
             pltpu.VMEM(square, narrow),
+            pltpu.VMEM((2 * (states // times), states), narrow),
+            pltpu.VMEM(square, narrow),
             pltpu.VMEM(square, narrow),
             pltpu.VMEM(square, narrow),
             pltpu.VMEM(square, narrow),
             pltpu.VMEM(square, narrow),
             pltpu.VMEM(square, wide),
             pltpu.VMEM((times, states // times, states), narrow),
+            pltpu.VMEM((times, SUBLANES, LANES), wide),
             dma((2,)),
             dma((2,)),
-            dma((times, 2)),
-            dma((times, 2)),
+            dma((times,)),
+            dma((times,)),
+            dma((times,)),
+            dma((times,)),
+            dma((times, PARTS)),
+            dma((times, PARTS)),
             dma((times,)),
             dma((times,)),
             dma((times,)),
@@ -434,7 +518,7 @@
         and times > 2
         and times & (times - 1) == 0
         and states % (times * ROW_TILE) == 0
-        and states % (2 * ROW_TILE) == 0
+        and states % (PARTS * ROW_TILE) == 0
         and states % LANES == 0
     )
     chosen = fused_device if fits else general_device

time: 61.2 us -> 61.2 us (level)
  no operation moved by 1% of the time
where the time goes in v2:
time: 61.2 us; the launch traced here: 60.7 us
  Pallas kernels  56.6 us (92%)
  local copies, waits for them, and re-layouts  2.11 us (3%)
  between operations  1.95 us (3%)
    pallas_call x1, Pallas kernels, fused_device(): pl.pallas_call(functools.partial(fused_kernel, times, lax.axis_size('sect...  56.6 us
    unnamed x1, local copies, waits for them, and re-layouts  2.11 us

profile of v2, /device:TPU:0, one launch (start us, length us, event | category | flops | bytes accessed | tf_op | source)
XLA Modules:
  0.0 60.7 jit_solution(3671128849414530466)
XLA Ops:
  1.9 56.6 %shard_map.64 = bf16[1,1,640,640]{3,2,1,0:T(8,128)(2,1)} custom-call(s32[1]{0:T(128)S(6)} %copy.10.size_ref, f32[1]{0:T(128)S(6)} %copy.8.particle_ref, f32[1]{0:T(128)S(6)} %copy.9.hole_ref, bf16[1,1,640,640]{3,2,1,0:T(8,128)(2,1)} %prop_ref.1, bf16[1,640,640]{2,1,0:T(8,128)(2,1)} %operator_ref.1, f32[1,640]{1,0:T(1,128)} %energy_ref.1), custom_call_target="tpu_custom_call" | custom-call | tf_op jit(solution)/shard_map/pallas_call | solution.py:476
  58.6 2.1 %copy.11 = bf16[1,1,640,640]{3,2,1,0:T(8,128)(2,1)} copy(bf16[1,1,640,640]{3,2,1,0:T(8,128)(2,1)} %shard_map.64) | data formatting | bytes 1638400

commit v3 on v2

--- a/solution.py
+++ b/solution.py
@@ -505,7 +505,7 @@
             dma((times,)),
         ],
         compiler_params=pltpu.CompilerParams(
-            collective_id=0, has_side_effects=True, vmem_limit_bytes=60 * 2**20
+            collective_id=0, has_side_effects=True, vmem_limit_bytes=28 * 2**20
         ),
     )(sector_sizes, hyb_particle, hyb_hole, propagator, rising_op, energies)
 

time: 61.2 us -> 60.1 us (0.982)
  Pallas kernels: 56.6 us -> 54.3 us
  local copies, waits for them, and re-layouts: 2.11 us -> 3.18 us
    pallas_call x1, Pallas kernels: 56.6 us -> 54.3 us  [fused_device(): pl.pallas_call(functools.partial(fused_kernel, times, lax.axis_size('sect...]
    unnamed x1 -> x7, local copies, waits for them, and re-layouts: 2.11 us -> 3.18 us
where the time goes in v3:
time: 60.1 us; the launch traced here: 59.5 us
  Pallas kernels  54.3 us (90%)
  local copies, waits for them, and re-layouts  3.18 us (5%)
  between operations  1.98 us (3%)
    pallas_call x1, Pallas kernels, fused_device(): pl.pallas_call(functools.partial(fused_kernel, times, lax.axis_size('sect...  54.3 us
    unnamed x7, local copies, waits for them, and re-layouts  3.18 us

profile of v3, /device:TPU:0, one launch (start us, length us, event | category | flops | bytes accessed | tf_op | source)
XLA Modules:
  0.0 59.5 jit_solution(17631239105342948842)
XLA Ops:
  0.0 0.0 copy-start.2
  2.0 0.0 copy-done.2
  2.0 0.0 copy-start
  2.0 1.1 %copy-done = bf16[1,1,640,640]{3,2,1,0:T(8,128)(2,1)S(1)} copy-done((bf16[1,1,640,640]{3,2,1,0:T(8,128)(2,1)S(1)}, bf16[1,1,640,640]{3,2,1,0:T(8,128)(2,1)}, u32[]{:S(2)}) %copy-start) | copy-done | bytes 819224
  3.1 0.0 copy-start.1
  3.1 1.1 %copy-done.1 = bf16[1,640,640]{2,1,0:T(8,128)(2,1)S(1)} copy-done((bf16[1,640,640]{2,1,0:T(8,128)(2,1)S(1)}, bf16[1,640,640]{2,1,0:T(8,128)(2,1)}, u32[]{:S(2)}) %copy-start.1) | copy-done | bytes 819224
  4.3 54.3 %shard_map.64 = bf16[1,1,640,640]{3,2,1,0:T(8,128)(2,1)S(1)} custom-call(s32[1]{0:T(128)S(6)} %copy.10.size_ref, f32[1]{0:T(128)S(6)} %copy.8.particle_ref, f32[1]{0:T(128)S(6)} %copy.9.hole_ref, bf16[1,1,640,640]{3,2,1,0:T(8,128)(2,1)S(1)} %copy-done, bf16[1,640,640]{2,1,0:T(8,128)(2,1)S(1)} %copy-done.1, f32[1,640]{1,0:T(1,128)S(1)} %copy-done.2), custom_call_target="tpu_custom_call" | custom-call | tf_op jit(solution)/shard_map/pallas_call | solution.py:476
  58.6 0.9 %copy.11 = bf16[1,1,640,640]{3,2,1,0:T(8,128)(2,1)} copy(bf16[1,1,640,640]{3,2,1,0:T(8,128)(2,1)S(1)} %shard_map.64) | data formatting | bytes 1638400
Async XLA Ops:
  0.0 2.0 %copy-start.2 = (f32[1,640]{1,0:T(1,128)S(1)}, f32[1,640]{1,0:T(1,128)}, u32[]{:S(2)}) copy-start(f32[1,640]{1,0:T(1,128)} %energy_ref.1) | copy-start | bytes 7684
  2.0 1.1 %copy-start = (bf16[1,1,640,640]{3,2,1,0:T(8,128)(2,1)S(1)}, bf16[1,1,640,640]{3,2,1,0:T(8,128)(2,1)}, u32[]{:S(2)}) copy-start(bf16[1,1,640,640]{3,2,1,0:T(8,128)(2,1)} %prop_ref.1) | copy-start | bytes 2457604
  3.1 1.1 %copy-start.1 = (bf16[1,640,640]{2,1,0:T(8,128)(2,1)S(1)}, bf16[1,640,640]{2,1,0:T(8,128)(2,1)}, u32[]{:S(2)}) copy-start(bf16[1,640,640]{2,1,0:T(8,128)(2,1)} %operator_ref.1) | copy-start | bytes 2457604
